TPU v7x, 32 devices: a whole 2x2x4 slice. The times are simulated.
32 devices in a mesh: groups: 2 (over x), rows: 16 (over z, y, core).
Axes of the slice: x: 2, y: 2, z: 4, core: 2. Of those that a mesh axis runs over, the one named last changes fastest.
Arguments:
- frames: bfloat16 [2048, 3, 256], P(('groups', 'rows')), parts along dimension 0, may hold values from -6 to 6
- conv_tiles: bfloat16 [16, 27, 512, 128], P('rows'), may hold values from -0.0390625 to 0.0390625
- up_tiles: bfloat16 [16, 9, 256, 128], P('rows'), may hold values from -0.0625 to 0.0625
Outputs:
- upsampled_tiles: bfloat16 [32, 256, 128], P(('groups', 'rows')), parts along dimension 0
There are 2 independent parts, one for each index of `groups`. A program takes and returns all parts, laid end to end along the dimension named above; an argument that names none is the same for every part. Nothing has to cross between parts.
All inputs are finite; a program needn't handle non-finite values.
Results may differ from a plain program's by a relative error of at most 0.009.
Values may be sent and summed in bfloat16 or wider, within the bound.
A program may use at most 64 MiB of HBM per device.

v0:
```python
import jax
import jax.numpy as jnp
from jax import lax
from jax.sharding import PartitionSpec as P

W = 64


def partner_2(block, axis, stride):
    count = lax.axis_size(axis)
    route = []
    for low in range(count):
        high = low | 1 << stride
        if high != low and high < count:
            route += [(low, high), (high, low)]
    return lax.ppermute(block, axis, route)


def shift_plane(planes, row_step, col_step):
    height = planes.shape[-2]
    width = planes.shape[-1]
    padded = jnp.pad(planes, [(0, 0)] * (planes.ndim - 2) + [(1, 1), (1, 1)])
    return padded[..., 1 + row_step : 1 + row_step + height, 1 + col_step : 1 + col_step + width]


def phase_groups(phase):
    if phase == 0:
        return [(-1, (0,)), (0, (1, 2))]
    return [(0, (0, 1)), (1, (2,))]


def upper_side(device_index, level):
    return device_index >> level & 1 == 1


def collect_channels(pieces, device_index):
    for level in range(3):
        partner = partner_2(pieces, "rows", level)
        pieces = jnp.where(
            upper_side(device_index, level),
            jnp.concatenate([partner, pieces], 0),
            jnp.concatenate([pieces, partner], 0),
        )
    return pieces


def halve_partials(totals, device_index, levels):
    for level in levels:
        middle = totals.shape[1] // 2
        upper_half = upper_side(device_index, level)
        kept_part = jnp.where(upper_half, totals[:, middle:], totals[:, :middle])
        sent_part = jnp.where(upper_half, totals[:, :middle], totals[:, middle:])
        totals = kept_part + partner_2(sent_part, "rows", level)
    return totals


def halve_outputs(totals, device_index):
    for level in (2, 1, 0):
        middle = totals.shape[1] // 2
        upper_half = upper_side(device_index, level)
        kept_part = jnp.where(upper_half, totals[:, middle:], totals[:, :middle])
        sent_part = jnp.where(upper_half, totals[:, :middle], totals[:, middle:])
        totals = kept_part + partner_2(sent_part.astype(jnp.bfloat16), "rows", level).astype(
            sent_part.dtype
        )
    return totals


def on_device(frames, conv_tiles, up_tiles):
    device_index = lax.axis_index("rows")
    bit_count = lax.axis_size("rows").bit_length() - 1
    pieces = collect_channels(frames, device_index)
    in_channels = pieces.shape[0]
    voxels = pieces.shape[2]
    height = voxels // W
    volume = pieces.reshape(in_channels, 3, height, W)
    filters = conv_tiles.shape[3]
    partial_value = jnp.zeros((filters, voxels), jnp.float32)
    for time_tap in range(3):
        planes = []
        for spatial_tap in range(9):
            row_tap = spatial_tap // 3
            col_tap = spatial_tap % 3
            planes.append(
                shift_plane(volume[:, time_tap], row_tap - 1, col_tap - 1).reshape(
                    in_channels, voxels
                )
            )
        columns = jnp.concatenate(planes, 0)
        weights = conv_tiles[0, 9 * time_tap : 9 * time_tap + 9].reshape(9 * in_channels, filters)
        partial_value = partial_value + lax.dot_general(
            weights, columns, (((0,), (0,)), ((), ())), preferred_element_type=jnp.float32
        )
    summed = halve_partials(partial_value, device_index, list(range(bit_count - 1, 2, -1)))
    hidden_block = jax.nn.silu(summed).astype(jnp.bfloat16)
    for level in range(3, bit_count):
        partner = partner_2(hidden_block, "rows", level)
        hidden_block = jnp.where(
            upper_side(device_index, level),
            jnp.concatenate([partner, hidden_block], 1),
            jnp.concatenate([hidden_block, partner], 1),
        )
    hidden_planes = hidden_block.reshape(filters, height, W)
    up_weight = up_tiles[0].astype(jnp.float32)
    out_channels = up_weight.shape[1]
    phase_rows = []
    for row_phase in range(2):
        phase_cols = []
        for col_phase in range(2):
            weight_parts = []
            plane_parts = []
            for row_shift, row_taps in phase_groups(row_phase):
                for col_shift, col_taps in phase_groups(col_phase):
                    combined = jnp.zeros((out_channels, filters), jnp.float32)
                    for row_tap in row_taps:
                        for col_tap in col_taps:
                            combined = combined + up_weight[3 * row_tap + col_tap]
                    weight_parts.append(combined.astype(jnp.bfloat16))
                    plane_parts.append(
                        shift_plane(hidden_planes, row_shift, col_shift).reshape(filters, voxels)
                    )
            stacked_weight = jnp.concatenate(weight_parts, 1)
            stacked_planes = jnp.concatenate(plane_parts, 0)
            phase_out = jnp.dot(stacked_weight, stacked_planes, preferred_element_type=jnp.float32)
            phase_cols.append(phase_out.reshape(out_channels, height, W))
        phase_rows.append(jnp.stack(phase_cols, 0))
    phased = jnp.stack(phase_rows, 0)
    result = phased.transpose(2, 3, 0, 4, 1).reshape(out_channels, 4 * voxels)
    summed_out = halve_outputs(result, device_index)
    return summed_out.astype(jnp.bfloat16).reshape(1, out_channels, summed_out.shape[1])


def solution(mesh):
    return jax.shard_map(
        on_device,
        mesh=mesh,
        in_specs=(
            P(("groups", "rows"), None, None),
            P("rows", None, None, None),
            P("rows", None, None, None),
        ),
        out_specs=P(("groups", "rows"), None, None),
        check_vma=False,
    )
```

profile of v0, /device:TPU:0, one launch (start us, length us, event | category | flops | bytes accessed | tf_op | source)
XLA Modules:
  0.0 54.9 jit_solution(10346275166659987350)
XLA Ops:
  0.0 1.1 %copy.5 = bf16[64,3,256]{0,2,1:T(8,128)(2,1)S(1)} copy(bf16[64,3,256]{2,0,1:T(8,128)(2,1)} %param.3) | data formatting | bytes 196608 | tf_op args[0]
  1.1 0.6 %collective-permute-start = (bf16[64,3,256]{0,2,1:T(8,128)(2,1)S(1)}, bf16[64,3,256]{0,2,1:T(8,128)(2,1)S(1)}, u32[]{:S(2)}, u32[]{:S(2)}) collective-permute-start(bf16[64,3,256]{0,2,1:T(8,128)(2,1)S(1)} %copy.5), channel_id=1, source_target_pairs={{0,1},{1,0},{2,3},{3,2},{4,5},{5,4},{6,7},{7,6},{8,9},{9,8},{10,11... | collective-permute-start | bytes 294920 | tf_op jit(solution)/shard_map/ppermute | solution.py:16
  1.6 1.1 %convert_element_type.121 = f32[1,9,256,128]{3,2,1,0:T(8,128)S(1)} convert(bf16[1,9,256,128]{3,2,1,0:T(8,128)(2,1)} %param.5) | non-fusion elementwise | flops 294912 | bytes 1769472 | tf_op jit(solution)/shard_map/convert_element_type | solution.py:104
  2.8 0.0 collective-permute-done
  2.8 0.2 maximum_select_fusion.3
  3.0 2.8 %collective-permute-start.1 = (bf16[128,3,256]{0,2,1:T(8,128)(2,1)S(1)}, bf16[128,3,256]{0,2,1:T(8,128)(2,1)S(1)}, u32[]{:S(2)}, u32[]{:S(2)}) collective-permute-start(bf16[128,3,256]{0,2,1:T(8,128)(2,1)S(1)} %maximum_select_fusion.3), channel_id=1, source_target_pairs={{0,2},{2,0},{1,3},{3,1},{4,6},{6,4},{5,7},{7,5},{8,10},{10,8},{9,1... | collective-permute-start | bytes 589832 | tf_op jit(solution)/shard_map/ppermute | solution.py:16
  5.8 2.3 %fusion.74 = (bf16[1,9,512,128]{3,2,1,0:T(8,128)(2,1)S(1)}, bf16[1,9,512,128]{3,2,1,0:T(8,128)(2,1)S(1)}, bf16[1,9,512,128]{3,2,1,0:T(8,128)(2,1)S(1)}) fusion(bf16[1,27,512,128]{3,2,1,0:T(8,128)(2,1)} %param.4), kind=kLoop, calls=%fused_computation.175 | loop fusion | bytes 7077888 | tf_op jit(solution)/shard_map/slice | solution.py:90
  8.2 3.0 %collective-permute-done.1 = bf16[128,3,256]{0,2,1:T(8,128)(2,1)S(1)} collective-permute-done((bf16[128,3,256]{0,2,1:T(8,128)(2,1)S(1)}, bf16[128,3,256]{0,2,1:T(8,128)(2,1)S(1)}, u32[]{:S(2)}, u32[]{:S(2)}) %collective-permute-start.1) | collective-permute-done | bytes 196640 | tf_op jit(solution)/shard_map/ppermute | solution.py:16
  11.2 0.1 maximum_select_fusion.1
  11.3 1.9 %collective-permute-start.2 = (bf16[256,3,256]{0,2,1:T(8,128)(2,1)S(1)}, bf16[256,3,256]{0,2,1:T(8,128)(2,1)S(1)}, u32[]{:S(2)}, u32[]{:S(2)}) collective-permute-start(bf16[256,3,256]{0,2,1:T(8,128)(2,1)S(1)} %maximum_select_fusion.1), channel_id=1, source_target_pairs={{0,4},{4,0},{1,5},{5,1},{2,6},{6,2},{3,7},{7,3},{8,12},{12,8},{9,1... | collective-permute-start | bytes 1179656 | tf_op jit(solution)/shard_map/ppermute | solution.py:16
  13.2 0.1 fusion.68
  13.2 0.2 maximum_select_fusion.4
  13.5 0.1 maximum_select_fusion.2
  13.6 8.4 %collective-permute-done.2 = bf16[256,3,256]{0,2,1:T(8,128)(2,1)S(1)} collective-permute-done((bf16[256,3,256]{0,2,1:T(8,128)(2,1)S(1)}, bf16[256,3,256]{0,2,1:T(8,128)(2,1)S(1)}, u32[]{:S(2)}, u32[]{:S(2)}) %collective-permute-start.2) | collective-permute-done | bytes 393248 | tf_op jit(solution)/shard_map/ppermute | solution.py:16
  22.0 0.2 maximum_select_fusion
  22.3 0.2 fusion.75
  22.4 0.5 pad_slice_fusion
  23.0 0.2 pad_slice_fusion.16
  23.9 0.8 %fusion.76 = f32[256,128]{1,0:T(8,128)S(1)} fusion(bf16[4608,256]{0,1:T(8,128)(2,1)S(1)} %constant_dynamic-update-slice_fusion, bf16[4608,128]{1,0:T(8,128)(2,1)S(1)} %bitcast.170), kind=kOutput, calls=%fused_computation.177 | convolution fusion | flops 301989888 | bytes 3670016 | tf_op jit(solution)/shard_map/dot_general | solution.py:91
  24.7 0.8 %convolution_add_fusion.1 = f32[256,128]{1,0:T(8,128)S(1)} fusion(f32[256,128]{1,0:T(8,128)S(1)} %fusion.76, bf16[4608,256]{0,1:T(8,128)(2,1)S(1)} %constant_dynamic-update-slice_fusion.9, bf16[4608,128]{1,0:T(8,128)(2,1)S(1)} %bitcast.172), kind=kOutput, calls=%fused_computation.2 | convolution fusion | flops 302022656 | bytes 3801088 | tf_op jit(solution)/shard_map/dot_general | solution.py:91
  25.5 0.8 %fusion = f32[128,256]{0,1:T(8,128)S(1)} fusion(f32[256,128]{1,0:T(8,128)S(1)} %convolution_add_fusion.1, bf16[4608,256]{0,1:T(8,128)(2,1)S(1)} %constant_dynamic-update-slice_fusion.18, bf16[4608,128]{1,0:T(8,128)(2,1)S(1)} %bitcast.171), kind=kOutput, calls=%fused_computation.1 | convolution fusion | flops 302022656 | bytes 3801088 | tf_op jit(solution)/shard_map/dot_general | solution.py:91
  26.4 2.6 %collective-permute-start.3 = (f32[128,128]{0,1:T(8,128)S(1)}, f32[128,128]{0,1:T(8,128)S(1)}, u32[]{:S(2)}, u32[]{:S(2)}) collective-permute-start(f32[128,128]{0,1:T(8,128)S(1)} %slice_select_fusion), channel_id=1, source_target_pairs={{0,8},{8,0},{1,9},{9,1},{2,10},{10,2},{3,11},{11,3},{4,12},{12,4},... | collective-permute-start | bytes 196616 | tf_op jit(solution)/shard_map/ppermute | solution.py:16
  28.9 0.1 add_convert_fusion.10
  29.0 2.6 %collective-permute-done.3 = f32[128,128]{0,1:T(8,128)S(1)} collective-permute-done((f32[128,128]{0,1:T(8,128)S(1)}, f32[128,128]{0,1:T(8,128)S(1)}, u32[]{:S(2)}, u32[]{:S(2)}) %collective-permute-start.3) | collective-permute-done | bytes 65568 | tf_op jit(solution)/shard_map/ppermute | solution.py:16
  31.6 2.7 %collective-permute-start.4 = (bf16[128,128]{0,1:T(8,128)(2,1)S(1)}, bf16[128,128]{0,1:T(8,128)(2,1)S(1)}, u32[]{:S(2)}, u32[]{:S(2)}) collective-permute-start(bf16[128,128]{0,1:T(8,128)(2,1)S(1)} %multiply_convert_fusion), channel_id=1, source_target_pairs={{0,8},{8,0},{1,9},{9,1},{2,10},{10,2},{3,11},{11,3},{4,12},{12,4},... | collective-permute-start | bytes 98312 | tf_op jit(solution)/shard_map/ppermute | solution.py:16
  34.3 2.2 %collective-permute-done.4 = bf16[128,128]{0,1:T(8,128)(2,1)S(1)} collective-permute-done((bf16[128,128]{0,1:T(8,128)(2,1)S(1)}, bf16[128,128]{0,1:T(8,128)(2,1)S(1)}, u32[]{:S(2)}, u32[]{:S(2)}) %collective-permute-start.4) | collective-permute-done | bytes 32800 | tf_op jit(solution)/shard_map/ppermute | solution.py:16
  36.5 0.1 pad_slice_fusion.31
  36.6 0.3 fusion.1
  36.9 0.3 copy.9
  37.2 0.3 fusion.16
  37.5 0.3 copy.10
  37.7 0.3 fusion.31
  38.0 0.3 copy.11
  38.3 0.3 fusion.46
  38.6 0.3 copy.12
  38.8 0.5 maximum_bitcast_fusion.1
  39.3 0.5 maximum_bitcast_fusion.2
  39.8 0.5 maximum_bitcast_fusion
  40.4 0.7 %reshape.195 = f32[256,1024]{0,1:T(8,128)S(1)} reshape(f32[256,4,2,64,2]{0,4,3,2,1:T(2,128)S(1)} %maximum_bitcast_fusion) | data formatting | bytes 2097152 | tf_op jit(solution)/shard_map/reshape | solution.py:128
  41.1 0.1 select_convert_fusion
  41.1 1.8 %collective-permute-start.5 = (bf16[256,512]{0,1:T(8,128)(2,1)S(1)}, bf16[256,512]{0,1:T(8,128)(2,1)S(1)}, u32[]{:S(2)}, u32[]{:S(2)}) collective-permute-start(bf16[256,512]{0,1:T(8,128)(2,1)S(1)} %select_convert_fusion), channel_id=1, source_target_pairs={{0,4},{4,0},{1,5},{5,1},{2,6},{6,2},{3,7},{7,3},{8,12},{12,8},{9,1... | collective-permute-start | bytes 786440 | tf_op jit(solution)/shard_map/ppermute | solution.py:16
  43.0 4.6 %collective-permute-done.5 = bf16[256,512]{0,1:T(8,128)(2,1)S(1)} collective-permute-done((bf16[256,512]{0,1:T(8,128)(2,1)S(1)}, bf16[256,512]{0,1:T(8,128)(2,1)S(1)}, u32[]{:S(2)}, u32[]{:S(2)}) %collective-permute-start.5) | collective-permute-done | bytes 262176 | tf_op jit(solution)/shard_map/ppermute | solution.py:16
  47.6 0.1 convert_add_fusion
  47.7 1.5 %collective-permute-start.6 = (bf16[256,256]{0,1:T(8,128)(2,1)S(1)}, bf16[256,256]{0,1:T(8,128)(2,1)S(1)}, u32[]{:S(2)}, u32[]{:S(2)}) collective-permute-start(bf16[256,256]{0,1:T(8,128)(2,1)S(1)} %select_convert_fusion.1), channel_id=1, source_target_pairs={{0,2},{2,0},{1,3},{3,1},{4,6},{6,4},{5,7},{7,5},{8,10},{10,8},{9,1... | collective-permute-start | bytes 393224 | tf_op jit(solution)/shard_map/ppermute | solution.py:16
  49.2 3.5 %collective-permute-done.6 = bf16[256,256]{0,1:T(8,128)(2,1)S(1)} collective-permute-done((bf16[256,256]{0,1:T(8,128)(2,1)S(1)}, bf16[256,256]{0,1:T(8,128)(2,1)S(1)}, u32[]{:S(2)}, u32[]{:S(2)}) %collective-permute-start.6) | collective-permute-done | bytes 131104 | tf_op jit(solution)/shard_map/ppermute | solution.py:16
  52.8 0.1 collective-permute-start.7
  52.9 1.2 %collective-permute-done.7 = bf16[256,128]{0,1:T(8,128)(2,1)S(1)} collective-permute-done((bf16[256,128]{0,1:T(8,128)(2,1)S(1)}, bf16[256,128]{0,1:T(8,128)(2,1)S(1)}, u32[]{:S(2)}, u32[]{:S(2)}) %collective-permute-start.7) | collective-permute-done | bytes 65568 | tf_op jit(solution)/shard_map/ppermute | solution.py:16
  54.2 0.7 %copy.13 = bf16[1,256,128]{2,1,0:T(8,128)(2,1)} copy(bf16[1,256,128]{1,2,0:T(8,128)(2,1)S(1)} %fusion.67) | data formatting | bytes 131072 | tf_op jit(solution)/shard_map/reshape | solution.py:130
  (36 shorter events, 0.7 us)
Async XLA Ops:
  1.1 1.7 %collective-permute-start = (bf16[64,3,256]{0,2,1:T(8,128)(2,1)S(1)}, bf16[64,3,256]{0,2,1:T(8,128)(2,1)S(1)}, u32[]{:S(2)}, u32[]{:S(2)}) collective-permute-start(bf16[64,3,256]{0,2,1:T(8,128)(2,1)S(1)} %copy.5), channel_id=1, source_target_pairs={{0,1},{1,0},{2,3},{3,2},{4,5},{5,4},{6,7},{7,6},{8,9},{9,8},{10,11... | collective-permute-start | bytes 294920 | tf_op jit(solution)/shard_map/ppermute | solution.py:16
  3.0 8.1 %collective-permute-start.1 = (bf16[128,3,256]{0,2,1:T(8,128)(2,1)S(1)}, bf16[128,3,256]{0,2,1:T(8,128)(2,1)S(1)}, u32[]{:S(2)}, u32[]{:S(2)}) collective-permute-start(bf16[128,3,256]{0,2,1:T(8,128)(2,1)S(1)} %maximum_select_fusion.3), channel_id=1, source_target_pairs={{0,2},{2,0},{1,3},{3,1},{4,6},{6,4},{5,7},{7,5},{8,10},{10,8},{9,1... | collective-permute-start | bytes 589832 | tf_op jit(solution)/shard_map/ppermute | solution.py:16
  11.3 10.8 %collective-permute-start.2 = (bf16[256,3,256]{0,2,1:T(8,128)(2,1)S(1)}, bf16[256,3,256]{0,2,1:T(8,128)(2,1)S(1)}, u32[]{:S(2)}, u32[]{:S(2)}) collective-permute-start(bf16[256,3,256]{0,2,1:T(8,128)(2,1)S(1)} %maximum_select_fusion.1), channel_id=1, source_target_pairs={{0,4},{4,0},{1,5},{5,1},{2,6},{6,2},{3,7},{7,3},{8,12},{12,8},{9,1... | collective-permute-start | bytes 1179656 | tf_op jit(solution)/shard_map/ppermute | solution.py:16
  26.4 5.2 %collective-permute-start.3 = (f32[128,128]{0,1:T(8,128)S(1)}, f32[128,128]{0,1:T(8,128)S(1)}, u32[]{:S(2)}, u32[]{:S(2)}) collective-permute-start(f32[128,128]{0,1:T(8,128)S(1)} %slice_select_fusion), channel_id=1, source_target_pairs={{0,8},{8,0},{1,9},{9,1},{2,10},{10,2},{3,11},{11,3},{4,12},{12,4},... | collective-permute-start | bytes 196616 | tf_op jit(solution)/shard_map/ppermute | solution.py:16
  31.6 4.9 %collective-permute-start.4 = (bf16[128,128]{0,1:T(8,128)(2,1)S(1)}, bf16[128,128]{0,1:T(8,128)(2,1)S(1)}, u32[]{:S(2)}, u32[]{:S(2)}) collective-permute-start(bf16[128,128]{0,1:T(8,128)(2,1)S(1)} %multiply_convert_fusion), channel_id=1, source_target_pairs={{0,8},{8,0},{1,9},{9,1},{2,10},{10,2},{3,11},{11,3},{4,12},{12,4},... | collective-permute-start | bytes 98312 | tf_op jit(solution)/shard_map/ppermute | solution.py:16
  41.1 6.4 %collective-permute-start.5 = (bf16[256,512]{0,1:T(8,128)(2,1)S(1)}, bf16[256,512]{0,1:T(8,128)(2,1)S(1)}, u32[]{:S(2)}, u32[]{:S(2)}) collective-permute-start(bf16[256,512]{0,1:T(8,128)(2,1)S(1)} %select_convert_fusion), channel_id=1, source_target_pairs={{0,4},{4,0},{1,5},{5,1},{2,6},{6,2},{3,7},{7,3},{8,12},{12,8},{9,1... | collective-permute-start | bytes 786440 | tf_op jit(solution)/shard_map/ppermute | solution.py:16
  47.7 5.0 %collective-permute-start.6 = (bf16[256,256]{0,1:T(8,128)(2,1)S(1)}, bf16[256,256]{0,1:T(8,128)(2,1)S(1)}, u32[]{:S(2)}, u32[]{:S(2)}) collective-permute-start(bf16[256,256]{0,1:T(8,128)(2,1)S(1)} %select_convert_fusion.1), channel_id=1, source_target_pairs={{0,2},{2,0},{1,3},{3,1},{4,6},{6,4},{5,7},{7,5},{8,10},{10,8},{9,1... | collective-permute-start | bytes 393224 | tf_op jit(solution)/shard_map/ppermute | solution.py:16
  52.8 1.3 %collective-permute-start.7 = (bf16[256,128]{0,1:T(8,128)(2,1)S(1)}, bf16[256,128]{0,1:T(8,128)(2,1)S(1)}, u32[]{:S(2)}, u32[]{:S(2)}) collective-permute-start(bf16[256,128]{0,1:T(8,128)(2,1)S(1)} %select_convert_fusion.2), channel_id=1, source_target_pairs={{0,1},{1,0},{2,3},{3,2},{4,5},{5,4},{6,7},{7,6},{8,9},{9,8},{10,11... | collective-permute-start | bytes 196616 | tf_op jit(solution)/shard_map/ppermute | solution.py:16
where the time goes:
time: 55.1 us; the launch traced here: 54.9 us
  waiting for transfers between devices  25.5 us (46%)
  starting transfers between devices  13.9 us (25%)
  local copies, waits for them, and re-layouts  7.49 us (14%)
  other arithmetic  4.05 us (7%)
  matrix products  3.45 us (6%)
    ppermute x8, waiting for transfers between devices, partner_2(): return lax.ppermute(block, axis, route)  25.5 us
    ppermute x8, starting transfers between devices, partner_2(): return lax.ppermute(block, axis, route)  13.9 us
    dot_general x3, matrix products, on_device(): lax.dot_general(weights, columns, (((0,), (0,)), ((), ())), preferred_ele...  2.39 us
    slice x1, local copies, waits for them, and re-layouts, on_device(): conv_tiles[0, 9 * time_tap:9 * time_tap + 9]  2.35 us
    unnamed x25, local copies, waits for them, and re-layouts  1.52 us
    convert_element_type x1, other arithmetic, on_device(): up_weight = up_tiles[0].astype(jnp.float32)  1.15 us
  transfers between devices with their start and end apart: 8, of which 7 were waited for; matrix products, arithmetic and copies ran while one was open for 7% of the time, Pallas kernels for 0%

commit v1 on v0

--- a/solution.py
+++ b/solution.py
@@ -1,6 +1,8 @@
 import jax
 import jax.numpy as jnp
 from jax import lax
+from jax.experimental import pallas as pl
+from jax.experimental.pallas import tpu as pltpu
 from jax.sharding import PartitionSpec as P
 
 W = 64
@@ -130,9 +132,271 @@
     return summed_out.astype(jnp.bfloat16).reshape(1, out_channels, summed_out.shape[1])
 
 
+MESH = pl.DeviceIdType.MESH
+
+
+def fused_kernel(
+    frames_ref, conv_hbm, up_hbm, out_ref,
+    xg, wbuf, upbuf, pw, zacc, partial, pbuf, prx, hp, ownp, sbuf, crx, rbuf, rrx,
+    lsem, gs, gr, ps, pr, cs_, cr, rs, rr,
+):
+    me = lax.axis_index("rows")
+    f = lax.rem(me, 8)
+    half = me // 8
+    c = lax.rem(f, 2)
+    y = lax.rem(f // 2, 2)
+    z = f // 4
+    dc, dy, dz = 1 - 2 * c, 2 - 4 * y, 4 - 8 * z
+    pc, py, pz, pd = me + dc, me + dy, me + dz, me + dy + dz
+    far = me + 8 - 16 * half
+    shard, _, voxels = frames_ref.shape
+    height = voxels // W
+    depth = wbuf.shape[1] // 2
+    filters = wbuf.shape[2]
+    piece = shard // 2
+
+    def weight_copy(k, which):
+        rows = pl.ds(pl.multiple_of(which * depth, depth), depth)
+        return pltpu.make_async_copy(conv_hbm.at[0, :, rows, :], wbuf.at[:, rows, :], lsem.at[k])
+
+    w_near = weight_copy(0, z)
+    w_far = weight_copy(1, 1 - z)
+    up_copy = pltpu.make_async_copy(up_hbm.at[0], upbuf, lsem.at[2])
+
+    barrier = pltpu.get_barrier_semaphore()
+    for peer in (pc, py, pz, pd, far):
+        pl.semaphore_signal(barrier, inc=1, device_id={"rows": peer}, device_id_type=MESH)
+    w_near.start()
+    up_copy.start()
+    w_far.start()
+    for a in range(3):
+        xg[a, pl.ds(pl.multiple_of(f * shard, shard), shard), :] = frames_ref[:, a, :]
+    pl.semaphore_wait(barrier, 5)
+
+    def send(src, dst, ssem, rsem, k, peer):
+        return pltpu.make_async_remote_copy(
+            src_ref=src, dst_ref=dst, send_sem=ssem.at[k], recv_sem=rsem.at[k],
+            device_id={"rows": peer}, device_id_type=MESH,
+        )
+
+    def gather(k, slot, part, peer):
+        if part is None:
+            view = xg.at[:, pl.ds(pl.multiple_of(slot * shard, shard), shard), :]
+        else:
+            view = xg.at[:, pl.ds(pl.multiple_of(slot * shard + part * piece, piece), piece), :]
+        return send(view, view, gs, gr, k, peer)
+
+    sy, sz, sd = f + dy, f + dz, f + dy + dz
+    own_y0 = gather(0, f, 0, py)
+    own_z1 = gather(1, f, 1, pz)
+    own_y1 = gather(2, f, 1, py)
+    own_z0 = gather(3, f, 0, pz)
+    own_c = gather(4, f, None, pc)
+    for copy in (own_y0, own_z1, own_c, own_y1, own_z0):
+        copy.start()
+
+    up_copy.wait()
+    for p in range(2):
+        for q in range(2):
+            for k, (_, row_taps) in enumerate(phase_groups(p)):
+                for l, (_, col_taps) in enumerate(phase_groups(q)):
+                    total = None
+                    for b in row_taps:
+                        for e in col_taps:
+                            tap = upbuf[3 * b + e].astype(jnp.float32)
+                            total = tap if total is None else total + tap
+                    at = (2 * k + l) * filters
+                    pw[p, q, :, at : at + filters] = total.astype(jnp.bfloat16)
+
+    own_y0.wait_recv()
+    d_z0 = gather(5, sy, 0, pz)
+    d_z0.start()
+    y0_c = gather(6, sy, 0, pc)
+    y0_c.start()
+    own_z1.wait_recv()
+    d_y1 = gather(7, sz, 1, py)
+    d_y1.start()
+    z1_c = gather(8, sz, 1, pc)
+    z1_c.start()
+    own_y1.wait_recv()
+    y1_c = gather(9, sy, 1, pc)
+    y1_c.start()
+    own_z0.wait_recv()
+    z0_c = gather(10, sz, 0, pc)
+    z0_c.start()
+
+    def conv_half(which, first):
+        rows = pl.ds(pl.multiple_of(which * depth, depth), depth)
+        xt = jnp.concatenate([xg[a, rows, :].T for a in range(3)], axis=1)
+        for t in range(0, 9, 2):
+            taps = [t, t + 1] if t + 1 < 9 else [t]
+            rhs = jnp.concatenate(
+                [jnp.concatenate([wbuf[9 * a + tap, rows, :] for a in range(3)], 0) for tap in taps], 1
+            )
+            got = jnp.dot(xt, rhs, preferred_element_type=jnp.float32)
+            lanes = slice(t * filters, (t + len(taps)) * filters)
+            if first:
+                zacc[:, lanes] = got
+            else:
+                zacc[:, lanes] = zacc[:, lanes] + got
+
+    own_c.wait_recv()
+    y0_c.wait_recv()
+    y1_c.wait_recv()
+    w_near.wait()
+    conv_half(z, True)
+
+    d_z0.wait_recv()
+    d0_c = gather(11, sd, 0, pc)
+    d0_c.start()
+    d_y1.wait_recv()
+    d1_c = gather(12, sd, 1, pc)
+    d1_c.start()
+    z0_c.wait_recv()
+    z1_c.wait_recv()
+    w_far.wait()
+    d0_c.wait_recv()
+    d1_c.wait_recv()
+    conv_half(1 - z, False)
+
+    column = lax.rem(lax.broadcasted_iota(jnp.int32, (voxels, filters), 0), W)
+    at_left = column == 0
+    at_right = column == W - 1
+    blank = jnp.zeros((W, filters), jnp.float32)
+    sums = []
+    for e in range(3):
+        up_tap, mid_tap, low_tap = (
+            zacc[:, (3 * b + e) * filters : (3 * b + e + 1) * filters] for b in range(3)
+        )
+        sums.append(
+            mid_tap
+            + jnp.concatenate([blank, up_tap[: voxels - W]], 0)
+            + jnp.concatenate([low_tap[W:], blank], 0)
+        )
+    total = (
+        sums[1]
+        + jnp.where(at_left, 0.0, pltpu.roll(sums[0], 1, 0))
+        + jnp.where(at_right, 0.0, pltpu.roll(sums[2], voxels - 1, 0))
+    )
+    pbuf[...] = total.astype(jnp.bfloat16)
+    swap = send(pbuf, prx, ps, pr, 0, far)
+    swap.start()
+    partial[...] = total
+    edge = jnp.zeros((W, filters), jnp.bfloat16)
+    for s in range(3):
+        hp[s, :W, :] = edge
+        hp[s, W + voxels :, :] = edge
+    swap.wait_recv()
+    pre = partial[...] + prx[...].astype(jnp.float32)
+    hidden = (pre / (1.0 + jnp.exp(-pre))).astype(jnp.bfloat16).astype(jnp.float32)
+    inner = slice(W, W + voxels)
+    hp[0, inner, :] = jnp.where(at_left, 0.0, pltpu.roll(hidden, 1, 0)).astype(jnp.bfloat16)
+    hp[1, inner, :] = hidden.astype(jnp.bfloat16)
+    hp[2, inner, :] = jnp.where(at_right, 0.0, pltpu.roll(hidden, voxels - 1, 0)).astype(jnp.bfloat16)
+
+    def phase(p, target):
+        for q in range(2):
+            planes = jnp.concatenate(
+                [
+                    hp[q + l, pl.ds(pl.multiple_of((p + k) * W, W), voxels), :]
+                    for k in range(2)
+                    for l in range(2)
+                ],
+                1,
+            )
+            got = lax.dot_general(
+                planes, pw[p, q], (((1,), (1,)), ((), ())), preferred_element_type=jnp.float32
+            ).astype(target.dtype)
+            for row in range(height):
+                target[row, q * W : (q + 1) * W, :] = got[row * W : (row + 1) * W]
+
+    here = 2 * z + y
+    to_y = 2 * z + 1 - y
+    to_z = 2 * (1 - z) + y
+    to_d = 2 * (1 - z) + 1 - y
+    phase(1 - c, sbuf)
+    core = [send(sbuf.at[row], crx.at[row], cs_, cr, k, pc) for k, row in enumerate((to_d, to_z, to_y, here))]
+    for copy in core:
+        copy.start()
+    phase(c, ownp)
+    hops = []
+    for k, (row, peer) in enumerate(((to_d, pd), (to_z, pz), (to_y, py))):
+        core[k].wait_recv()
+        rbuf[k] = (ownp[row] + crx[row].astype(jnp.float32)).astype(jnp.bfloat16)
+        hop = send(rbuf.at[k], rrx.at[k], rs, rr, k, peer)
+        hop.start()
+        hops.append(hop)
+    core[3].wait_recv()
+    final = ownp[here] + crx[here].astype(jnp.float32)
+    for k in (2, 1, 0):
+        hops[k].wait_recv()
+        final = final + rrx[k].astype(jnp.float32)
+    from_row = lax.broadcasted_iota(jnp.int32, (2 * W, 2 * W), 0)
+    to_col = lax.broadcasted_iota(jnp.int32, (2 * W, 2 * W), 1)
+    place = (to_col == 2 * lax.rem(from_row, W) + from_row // W).astype(jnp.float32).astype(jnp.bfloat16)
+    out_ref[0] = lax.dot_general(
+        final.astype(jnp.bfloat16), place, (((0,), (0,)), ((), ())), preferred_element_type=jnp.float32
+    ).astype(jnp.bfloat16)
+    for copy in (
+        own_y0, own_z1, own_y1, own_z0, own_c, d_z0, y0_c, d_y1, z1_c, y1_c, z0_c, d0_c, d1_c,
+        swap, *core, *hops,
+    ):
+        copy.wait_send()
+
+
+def fused(frames, conv_tiles, up_tiles):
+    shard, _, voxels = frames.shape
+    _, taps, depth, filters = conv_tiles.shape
+    _, up_taps, outs, _ = up_tiles.shape
+    height = voxels // W
+    tile = 2 * W
+    bf, f32 = jnp.bfloat16, jnp.float32
+    dma = pltpu.SemaphoreType.DMA
+    return pl.pallas_call(
+        fused_kernel,
+        out_shape=jax.ShapeDtypeStruct((1, outs, tile), bf),
+        in_specs=[
+            pl.BlockSpec(memory_space=pltpu.VMEM),
+            pl.BlockSpec(memory_space=pl.ANY),
+            pl.BlockSpec(memory_space=pl.ANY),
+        ],
+        out_specs=pl.BlockSpec(memory_space=pltpu.VMEM),
+        scratch_shapes=[
+            pltpu.VMEM((3, depth, voxels), bf),
+            pltpu.VMEM((taps, depth, filters), bf),
+            pltpu.VMEM((up_taps, outs, filters), bf),
+            pltpu.VMEM((2, 2, outs, 4 * filters), bf),
+            pltpu.VMEM((voxels, 9 * filters), f32),
+            pltpu.VMEM((voxels, filters), f32),
+            pltpu.VMEM((voxels, filters), bf),
+            pltpu.VMEM((voxels, filters), bf),
+            pltpu.VMEM((3, voxels + 2 * W, filters), bf),
+            pltpu.VMEM((height, tile, outs), f32),
+            pltpu.VMEM((height, tile, outs), bf),
+            pltpu.VMEM((height, tile, outs), bf),
+            pltpu.VMEM((3, tile, outs), bf),
+            pltpu.VMEM((3, tile, outs), bf),
+            dma((3,)),
+            dma((13,)), dma((13,)),
+            dma((1,)), dma((1,)),
+            dma((4,)), dma((4,)),
+            dma((3,)), dma((3,)),
+        ],
+        compiler_params=pltpu.CompilerParams(collective_id=0, has_side_effects=True),
+    )(frames, conv_tiles, up_tiles)
+
+
+def route(frames, conv_tiles, up_tiles):
+    blocks = lax.axis_size("rows") // 8
+    tile_rows = frames.shape[2] // W // 4
+    if blocks == 2 and tile_rows == 1 and frames.shape[0] * 8 == conv_tiles.shape[2]:
+        return fused(frames, conv_tiles, up_tiles)
+    return on_device(frames, conv_tiles, up_tiles)
+
+
 def solution(mesh):
     return jax.shard_map(
-        on_device,
+        route,
         mesh=mesh,
         in_specs=(
             P(("groups", "rows"), None, None),

time: 55.1 us -> 28.6 us (0.52)
  waiting for transfers between devices: 25.5 us -> 0 us
  Pallas kernels: 0 us -> 25.3 us
  starting transfers between devices: 13.9 us -> 0 us
  local copies, waits for them, and re-layouts: 7.49 us -> 3.09 us
  other arithmetic: 4.05 us -> 0 us
  matrix products: 3.45 us -> 0 us
    ppermute x8 -> x0, waiting for transfers between devices: 25.5 us -> none  [partner_2(): return lax.ppermute(block, axis, route)]
    pallas_call x0 -> x1, Pallas kernels: none -> 25.3 us  [fused(): pl.pallas_call(fused_kernel, out_shape=jax.ShapeDtypeStruct((1, outs, til...]
    ppermute x8 -> x0, starting transfers between devices: 13.9 us -> none  [partner_2(): return lax.ppermute(block, axis, route)]
    dot_general x7 -> x0, matrix products: 3.45 us -> none  [the longest x3 2.39 us: on_device(): lax.dot_general(weights, columns, (((0,), (0,)), ((), ())), preferred_ele...]
    slice x5 -> x0, local copies, waits for them, and re-layouts: 3.34 us -> none  [the longest x1 2.35 us: on_device(): conv_tiles[0, 9 * time_tap:9 * time_tap + 9]]
    unnamed x25 -> x2, local copies, waits for them, and re-layouts: 1.52 us -> 3.09 us
    reshape x2 -> x0, local copies, waits for them, and re-layouts: 1.45 us -> none  [the longest x1 0.73 us: on_device(): summed_out.astype(jnp.bfloat16)]
    convert_element_type x7 -> x0, other arithmetic: 1.44 us -> none  [the longest x1 1.15 us: on_device(): up_weight = up_tiles[0].astype(jnp.float32)]
  transfers between devices with their start and end apart: 8 -> 0, of which waited for: 7 -> 0; matrix products, arithmetic and copies ran while one was open for 7% -> 0% of each run, Pallas kernels for 0% -> 0%
where the time goes in v1:
time: 28.6 us; the launch traced here: 28.4 us
  Pallas kernels  25.3 us (88%)
  local copies, waits for them, and re-layouts  3.09 us (11%)
    pallas_call x1, Pallas kernels, fused(): pl.pallas_call(fused_kernel, out_shape=jax.ShapeDtypeStruct((1, outs, til...  25.3 us
    unnamed x2, local copies, waits for them, and re-layouts  3.09 us

profile of v1, /device:TPU:0, one launch (start us, length us, event | category | flops | bytes accessed | tf_op | source)
XLA Modules:
  0.0 28.4 jit_solution(13824793145677535776)
XLA Ops:
  0.0 1.6 %copy.4.frames_ref = bf16[64,3,256]{2,1,0:T(4,128)(2,1)} copy(bf16[64,3,256]{2,0,1:T(8,128)(2,1)} %param.3) | data formatting | bytes 196608 | tf_op args[0]
  1.6 25.3 %shard_map.37 = bf16[1,256,128]{2,1,0:T(8,128)(2,1)} custom-call(bf16[64,3,256]{2,1,0:T(4,128)(2,1)} %copy.4.frames_ref, bf16[1,27,512,128]{3,2,1,0:T(8,128)(2,1)} %conv_hbm.1, bf16[1,9,256,128]{3,2,1,0:T(8,128)(2,1)} %up_hbm.1), custom_call_target="tpu_custom_call" | custom-call | tf_op jit(solution)/shard_map/pallas_call | solution.py:355
  26.9 1.5 %copy.6 = bf16[1,256,128]{2,1,0:T(8,128)(2,1)} copy(bf16[1,256,128]{2,1,0:T(8,128)(2,1)} %shard_map.37) | data formatting | bytes 131072

commit v2 on v1

--- a/solution.py
+++ b/solution.py
@@ -149,7 +149,7 @@
     dc, dy, dz = 1 - 2 * c, 2 - 4 * y, 4 - 8 * z
     pc, py, pz, pd = me + dc, me + dy, me + dz, me + dy + dz
     far = me + 8 - 16 * half
-    shard, _, voxels = frames_ref.shape
+    _, shard, voxels = frames_ref.shape
     height = voxels // W
     depth = wbuf.shape[1] // 2
     filters = wbuf.shape[2]
@@ -163,15 +163,18 @@
     w_far = weight_copy(1, 1 - z)
     up_copy = pltpu.make_async_copy(up_hbm.at[0], upbuf, lsem.at[2])
 
+    own_copy = pltpu.make_async_copy(
+        frames_ref, xg.at[:, pl.ds(pl.multiple_of(f * shard, shard), shard), :], lsem.at[3]
+    )
+    own_copy.start()
     barrier = pltpu.get_barrier_semaphore()
     for peer in (pc, py, pz, pd, far):
         pl.semaphore_signal(barrier, inc=1, device_id={"rows": peer}, device_id_type=MESH)
     w_near.start()
     up_copy.start()
     w_far.start()
-    for a in range(3):
-        xg[a, pl.ds(pl.multiple_of(f * shard, shard), shard), :] = frames_ref[:, a, :]
     pl.semaphore_wait(barrier, 5)
+    own_copy.wait()
 
     def send(src, dst, ssem, rsem, k, peer):
         return pltpu.make_async_remote_copy(
@@ -336,7 +339,7 @@
     place = (to_col == 2 * lax.rem(from_row, W) + from_row // W).astype(jnp.float32).astype(jnp.bfloat16)
     out_ref[0] = lax.dot_general(
         final.astype(jnp.bfloat16), place, (((0,), (0,)), ((), ())), preferred_element_type=jnp.float32
-    ).astype(jnp.bfloat16)
+    )
     for copy in (
         own_y0, own_z1, own_y1, own_z0, own_c, d_z0, y0_c, d_y1, z1_c, y1_c, z0_c, d0_c, d1_c,
         swap, *core, *hops,
@@ -354,9 +357,9 @@
     dma = pltpu.SemaphoreType.DMA
     return pl.pallas_call(
         fused_kernel,
-        out_shape=jax.ShapeDtypeStruct((1, outs, tile), bf),
+        out_shape=jax.ShapeDtypeStruct((1, outs, tile), f32),
         in_specs=[
-            pl.BlockSpec(memory_space=pltpu.VMEM),
+            pl.BlockSpec(memory_space=pl.ANY),
             pl.BlockSpec(memory_space=pl.ANY),
             pl.BlockSpec(memory_space=pl.ANY),
         ],
@@ -376,14 +379,14 @@
             pltpu.VMEM((height, tile, outs), bf),
             pltpu.VMEM((3, tile, outs), bf),
             pltpu.VMEM((3, tile, outs), bf),
-            dma((3,)),
+            dma((4,)),
             dma((13,)), dma((13,)),
             dma((1,)), dma((1,)),
             dma((4,)), dma((4,)),
             dma((3,)), dma((3,)),
         ],
         compiler_params=pltpu.CompilerParams(collective_id=0, has_side_effects=True),
-    )(frames, conv_tiles, up_tiles)
+    )(frames.transpose(1, 0, 2), conv_tiles, up_tiles).astype(bf)
 
 
 def route(frames, conv_tiles, up_tiles):

time: 28.6 us -> 26.1 us (0.913)
  local copies, waits for them, and re-layouts: 3.09 us -> 0 us
  other arithmetic: 0 us -> 1.54 us
  Pallas kernels: 25.3 us -> 24.4 us
    unnamed x2 -> x0, local copies, waits for them, and re-layouts: 3.09 us -> none
    convert_element_type x0 -> x1, other arithmetic: none -> 1.54 us  [fused(): return pl.pallas_call(fused_kernel, out_shape=jax.ShapeDtypeStruct((1, ou...]
    pallas_call x1, Pallas kernels: 25.3 us -> 24.4 us  [fused(): pl.pallas_call(fused_kernel, out_shape=jax.ShapeDtypeStruct((1, outs, til...]
where the time goes in v2:
time: 26.1 us; the launch traced here: 25.9 us
  Pallas kernels  24.4 us (93%)
  other arithmetic  1.54 us (6%)
    pallas_call x1, Pallas kernels, fused(): pl.pallas_call(fused_kernel, out_shape=jax.ShapeDtypeStruct((1, outs, til...  24.4 us
    convert_element_type x1, other arithmetic, fused(): return pl.pallas_call(fused_kernel, out_shape=jax.ShapeDtypeStruct((1, ou...  1.54 us

profile of v2, /device:TPU:0, one launch (start us, length us, event | category | flops | bytes accessed | tf_op | source)
XLA Modules:
  0.0 25.9 jit_solution(18102890506370014089)
XLA Ops:
  0.0 24.4 %shard_map.37 = f32[1,256,128]{2,1,0:T(8,128)} custom-call(bf16[3,64,256]{2,1,0:T(8,128)(2,1)} %bitcast.1, bf16[1,27,512,128]{3,2,1,0:T(8,128)(2,1)} %conv_hbm.1, bf16[1,9,256,128]{3,2,1,0:T(8,128)(2,1)} %up_hbm.1), custom_call_target="tpu_custom_call" | custom-call | tf_op jit(solution)/shard_map/pallas_call | solution.py:358
  24.4 1.5 %convert_element_type.3 = bf16[1,256,128]{2,1,0:T(8,128)(2,1)} convert(f32[1,256,128]{2,1,0:T(8,128)} %shard_map.37) | non-fusion elementwise | flops 32768 | bytes 196608 | tf_op jit(solution)/shard_map/convert_element_type | solution.py:389

commit v3 on v2

--- a/solution.py
+++ b/solution.py
@@ -138,7 +138,7 @@
 def fused_kernel(
     frames_ref, conv_hbm, up_hbm, out_ref,
     xg, wbuf, upbuf, pw, zacc, partial, pbuf, prx, hp, ownp, sbuf, crx, rbuf, rrx,
-    lsem, gs, gr, ps, pr, cs_, cr, rs, rr,
+    lsem, gs, gr, ps, pr, cs_, cr, rs, rr, ready,
 ):
     me = lax.axis_index("rows")
     f = lax.rem(me, 8)
@@ -168,12 +168,25 @@
     )
     own_copy.start()
     barrier = pltpu.get_barrier_semaphore()
-    for peer in (pc, py, pz, pd, far):
+    for peer in (pc, py, pz):
         pl.semaphore_signal(barrier, inc=1, device_id={"rows": peer}, device_id_type=MESH)
+    inner_chip = lax.rem(z + half, 2)
+    middle = inner_chip == 1
+    across = me + 4 - 8 * half
+
+    @pl.when(middle)
+    def _():
+        pl.semaphore_signal(barrier, inc=1, device_id={"rows": across}, device_id_type=MESH)
+
     w_near.start()
     up_copy.start()
     w_far.start()
-    pl.semaphore_wait(barrier, 5)
+    pl.semaphore_wait(barrier, 3 + inner_chip)
+
+    @pl.when(middle)
+    def _():
+        pl.semaphore_signal(ready, inc=1, device_id={"rows": across}, device_id_type=MESH)
+
     own_copy.wait()
 
     def send(src, dst, ssem, rsem, k, peer):
@@ -283,6 +296,11 @@
     )
     pbuf[...] = total.astype(jnp.bfloat16)
     swap = send(pbuf, prx, ps, pr, 0, far)
+
+    @pl.when(middle)
+    def _():
+        pl.semaphore_wait(ready, 1)
+
     swap.start()
     partial[...] = total
     edge = jnp.zeros((W, filters), jnp.bfloat16)
@@ -355,13 +373,14 @@
     tile = 2 * W
     bf, f32 = jnp.bfloat16, jnp.float32
     dma = pltpu.SemaphoreType.DMA
+    operands = (frames.transpose(1, 0, 2), conv_tiles, up_tiles)
     return pl.pallas_call(
         fused_kernel,
         out_shape=jax.ShapeDtypeStruct((1, outs, tile), f32),
         in_specs=[
-            pl.BlockSpec(memory_space=pl.ANY),
-            pl.BlockSpec(memory_space=pl.ANY),
-            pl.BlockSpec(memory_space=pl.ANY),
+            pl.BlockSpec(memory_space=pltpu.HBM),
+            pl.BlockSpec(memory_space=pltpu.HBM),
+            pl.BlockSpec(memory_space=pltpu.HBM),
         ],
         out_specs=pl.BlockSpec(memory_space=pltpu.VMEM),
         scratch_shapes=[
@@ -384,9 +403,12 @@
             dma((1,)), dma((1,)),
             dma((4,)), dma((4,)),
             dma((3,)), dma((3,)),
+            pltpu.SemaphoreType.REGULAR,
         ],
-        compiler_params=pltpu.CompilerParams(collective_id=0, has_side_effects=True),
-    )(frames.transpose(1, 0, 2), conv_tiles, up_tiles).astype(bf)
+        compiler_params=pltpu.CompilerParams(
+            collective_id=0, has_side_effects=True, vmem_limit_bytes=24 << 20
+        ),
+    )(*(pltpu.with_memory_space_constraint(x, pltpu.HBM) for x in operands)).astype(bf)
 
 
 def route(frames, conv_tiles, up_tiles):

time: 26.1 us -> 24.1 us (0.923)
  Pallas kernels: 24.4 us -> 23.3 us
  other arithmetic: 1.54 us -> 0.64 us
    pallas_call x1, Pallas kernels: 24.4 us -> 23.3 us  [fused(): pl.pallas_call(fused_kernel, out_shape=jax.ShapeDtypeStruct((1, outs, til...]
    convert_element_type x1, other arithmetic: 1.54 us -> 0.64 us  [fused(): return pl.pallas_call(fused_kernel, out_shape=jax.ShapeDtypeStruct((1, ou...]
where the time goes in v3:
time: 24.1 us; the launch traced here: 24 us
  Pallas kernels  23.3 us (97%)
  other arithmetic  0.64 us (3%)
    pallas_call x1, Pallas kernels, fused(): pl.pallas_call(fused_kernel, out_shape=jax.ShapeDtypeStruct((1, outs, til...  23.3 us
    convert_element_type x1, other arithmetic, fused(): return pl.pallas_call(fused_kernel, out_shape=jax.ShapeDtypeStruct((1, ou...  0.64 us

profile of v3, /device:TPU:0, one launch (start us, length us, event | category | flops | bytes accessed | tf_op | source)
XLA Modules:
  0.0 24.0 jit_solution(9321450696446678736)
XLA Ops:
  0.0 23.3 %shard_map.37 = f32[1,256,128]{2,1,0:T(8,128)S(1)} custom-call(bf16[3,64,256]{2,1,0:T(8,128)(2,1)} %bitcast.1, bf16[1,27,512,128]{3,2,1,0:T(8,128)(2,1)} %conv_hbm.1, bf16[1,9,256,128]{3,2,1,0:T(8,128)(2,1)} %up_hbm.1), custom_call_target="tpu_custom_call" | custom-call | tf_op jit(solution)/shard_map/pallas_call | solution.py:377
  23.3 0.6 %convert_element_type.3 = bf16[1,256,128]{2,1,0:T(8,128)(2,1)} convert(f32[1,256,128]{2,1,0:T(8,128)S(1)} %shard_map.37) | non-fusion elementwise | flops 32768 | bytes 196608 | tf_op jit(solution)/shard_map/convert_element_type | solution.py:411

commit v4 on v3

--- a/solution.py
+++ b/solution.py
@@ -166,7 +166,6 @@
     own_copy = pltpu.make_async_copy(
         frames_ref, xg.at[:, pl.ds(pl.multiple_of(f * shard, shard), shard), :], lsem.at[3]
     )
-    own_copy.start()
     barrier = pltpu.get_barrier_semaphore()
     for peer in (pc, py, pz):
         pl.semaphore_signal(barrier, inc=1, device_id={"rows": peer}, device_id_type=MESH)
@@ -178,6 +177,7 @@
     def _():
         pl.semaphore_signal(barrier, inc=1, device_id={"rows": across}, device_id_type=MESH)
 
+    own_copy.start()
     w_near.start()
     up_copy.start()
     w_far.start()
@@ -211,6 +211,10 @@
     for copy in (own_y0, own_z1, own_c, own_y1, own_z0):
         copy.start()
 
+    edge = jnp.zeros((W, filters), jnp.bfloat16)
+    for s in range(3):
+        hp[s, :W, :] = edge
+        hp[s, W + voxels :, :] = edge
     up_copy.wait()
     for p in range(2):
         for q in range(2):
@@ -303,10 +307,6 @@
 
     swap.start()
     partial[...] = total
-    edge = jnp.zeros((W, filters), jnp.bfloat16)
-    for s in range(3):
-        hp[s, :W, :] = edge
-        hp[s, W + voxels :, :] = edge
     swap.wait_recv()
     pre = partial[...] + prx[...].astype(jnp.float32)
     hidden = (pre / (1.0 + jnp.exp(-pre))).astype(jnp.bfloat16).astype(jnp.float32)
@@ -340,6 +340,9 @@
     for copy in core:
         copy.start()
     phase(c, ownp)
+    from_row = lax.broadcasted_iota(jnp.int32, (2 * W, 2 * W), 0)
+    to_col = lax.broadcasted_iota(jnp.int32, (2 * W, 2 * W), 1)
+    place = (to_col == 2 * lax.rem(from_row, W) + from_row // W).astype(jnp.float32).astype(jnp.bfloat16)
     hops = []
     for k, (row, peer) in enumerate(((to_d, pd), (to_z, pz), (to_y, py))):
         core[k].wait_recv()
@@ -352,9 +355,6 @@
     for k in (2, 1, 0):
         hops[k].wait_recv()
         final = final + rrx[k].astype(jnp.float32)
-    from_row = lax.broadcasted_iota(jnp.int32, (2 * W, 2 * W), 0)
-    to_col = lax.broadcasted_iota(jnp.int32, (2 * W, 2 * W), 1)
-    place = (to_col == 2 * lax.rem(from_row, W) + from_row // W).astype(jnp.float32).astype(jnp.bfloat16)
     out_ref[0] = lax.dot_general(
         final.astype(jnp.bfloat16), place, (((0,), (0,)), ((), ())), preferred_element_type=jnp.float32
     )

time: 24.1 us -> 24.1 us (level)
  no operation moved by 1% of the time
where the time goes in v4:
time: 24.1 us; the launch traced here: 24 us
  Pallas kernels  23.3 us (97%)
  other arithmetic  0.64 us (3%)
    pallas_call x1, Pallas kernels, fused(): pl.pallas_call(fused_kernel, out_shape=jax.ShapeDtypeStruct((1, outs, til...  23.3 us
    convert_element_type x1, other arithmetic, fused(): return pl.pallas_call(fused_kernel, out_shape=jax.ShapeDtypeStruct((1, ou...  0.64 us

profile of v4, /device:TPU:0, one launch (start us, length us, event | category | flops | bytes accessed | tf_op | source)
XLA Modules:
  0.0 24.0 jit_solution(3096587102325324353)
XLA Ops:
  0.0 23.3 %shard_map.37 = f32[1,256,128]{2,1,0:T(8,128)S(1)} custom-call(bf16[3,64,256]{2,1,0:T(8,128)(2,1)} %bitcast.1, bf16[1,27,512,128]{3,2,1,0:T(8,128)(2,1)} %conv_hbm.1, bf16[1,9,256,128]{3,2,1,0:T(8,128)(2,1)} %up_hbm.1), custom_call_target="tpu_custom_call" | custom-call | tf_op jit(solution)/shard_map/pallas_call | solution.py:377
  23.3 0.6 %convert_element_type.3 = bf16[1,256,128]{2,1,0:T(8,128)(2,1)} convert(f32[1,256,128]{2,1,0:T(8,128)S(1)} %shard_map.37) | non-fusion elementwise | flops 32768 | bytes 196608 | tf_op jit(solution)/shard_map/convert_element_type | solution.py:411
